TPU v7x, 128 devices: a whole 4x4x4 slice. The times are simulated.
128 devices in a mesh: rep: 16 (over x, y), exp: 8 (over z, core).
Axes of the slice: x: 4, y: 4, z: 4, core: 2. Of those that a mesh axis runs over, the one named last changes fastest.
Arguments:
- hidden: bfloat16 [16384, 4096], P(('rep', 'exp')), may hold values from -6 to 6
- parents: int32 [16384], P(('rep', 'exp')), may hold values from 0 to 1023
- routes: int32 [16384, 8], P(('rep', 'exp')), may hold values from 0 to 127, all different within a row; in each aligned block of 128 rows (0 to 127, 128 to 255, ...) at most 10 rows name the same one
- gates: float32 [16384, 8], P(('rep', 'exp')), may hold values from 0.05 to 1
- counts: int32 [128], P(('rep', 'exp')), may hold values from 64 to 128, as said below
- norm_gain: float32 [4096], replicated, may hold values from 0.1 to 1.9
- w_gate: bfloat16 [128, 4096, 768], P(('rep', 'exp')), may hold values from -0.09375 to 0.09375
- w_up: bfloat16 [128, 4096, 768], P(('rep', 'exp')), may hold values from -0.09375 to 0.09375
- w_down: bfloat16 [128, 768, 4096], P(('rep', 'exp')), may hold values from -0.21875 to 0.21875
Outputs:
- mixed: bfloat16 [16384, 4096], P(('rep', 'exp'))
Inputs may be any that keep to these rules, and one draw needn't show every extreme that they name: `routes`: in the rows of one device no expert is named more than 10 times. `counts`: some device has all of its rows live.
All inputs are finite; a program needn't handle non-finite values.
Results may differ from a plain program's by a relative error of at most 0.0071.
Values may be sent and summed in bfloat16 or wider, within the bound.
A program may use at most 128 MiB of HBM per device.

v0:
```python
import jax
import jax.numpy as jnp
from jax import lax
from jax.sharding import PartitionSpec as P


def run_expert(arrived, w_gate, w_up, w_down):
    gate_val = jnp.dot(arrived, w_gate[0], preferred_element_type=jnp.float32)
    up_val = jnp.dot(arrived, w_up[0], preferred_element_type=jnp.float32)
    act = (jax.nn.silu(gate_val) * up_val).astype(jnp.bfloat16)
    return jnp.dot(act, w_down[0], preferred_element_type=jnp.float32).astype(jnp.bfloat16)


def shards(hidden, parents, routes, gates, counts, norm_gain, w_gate, w_up, w_down):
    rows = hidden.shape[0]
    width = hidden.shape[1]
    top = routes.shape[1]
    n_rep = lax.axis_size("rep")
    n_exp = lax.axis_size("exp")
    n_dev = n_rep * n_exp
    cap = rows * top // n_dev + 2
    column = lax.axis_index("exp")
    micro = rows * n_exp
    per_expert = cap * n_exp
    slots = n_rep * per_expert
    live = jnp.arange(rows, dtype=jnp.int32) < counts[0]
    weights = gates / jnp.sum(gates, axis=1, keepdims=True) * live[:, None].astype(jnp.float32)
    flat = routes.reshape(-1)
    live_slot = jnp.repeat(live, top)
    onehot = (
        (flat[:, None] == jnp.arange(n_dev, dtype=jnp.int32)[None, :]) & live_slot[:, None]
    ).astype(jnp.int32)
    before = jnp.cumsum(onehot, axis=0) - onehot
    rank = jnp.sum(before * onehot, axis=1)
    position = jnp.where(live_slot, flat * cap + rank, n_dev * cap)
    slot_row = jnp.arange(rows * top, dtype=jnp.int32) // top
    match = position[:, None] == jnp.arange(n_dev * cap, dtype=jnp.int32)[None, :]
    filled_here = jnp.any(match, axis=0)
    row_here = jnp.sum(jnp.where(match, slot_row[:, None], 0), axis=0)
    parent_here = jnp.sum(jnp.where(match, jnp.repeat(parents, top)[:, None], 0), axis=0)
    w_here = jnp.sum(jnp.where(match, weights.reshape(-1)[:, None], 0.0), axis=0)
    table = jnp.stack(
        [
            jnp.where(filled_here, column * rows + row_here, -1).astype(jnp.float32),
            parent_here.astype(jnp.float32),
            w_here,
        ],
        axis=1,
    )
    group = lax.all_gather(hidden, "exp", axis=0, tiled=True)
    own = hidden.astype(jnp.float32)
    own_scale = lax.rsqrt(jnp.mean(own * own, axis=1) + 1e-06)
    scale_all = lax.all_gather(own_scale, "exp", axis=0, tiled=True)
    table_all = lax.all_gather(table.reshape(n_rep, n_exp, cap, 3), "exp", axis=1, tiled=False)
    table_col = lax.dynamic_index_in_dim(table_all, column, axis=2, keepdims=False)
    row_tbl = table_col[..., 0].astype(jnp.int32)
    src_row = table_col[..., 1].astype(jnp.int32).reshape(-1)
    w_tbl = table_col[..., 2]
    filled = (row_tbl >= 0).reshape(-1)
    src_key = jnp.where(filled, src_row, -1)
    choose = (src_key[:, None] == jnp.arange(micro, dtype=jnp.int32)[None, :]).astype(jnp.bfloat16)
    choose = lax.optimization_barrier(choose)
    key = table_col[..., 0].astype(jnp.int32).reshape(-1)
    w_key = table_col[..., 2].reshape(-1)
    pick = jnp.arange(micro, dtype=jnp.int32)[:, None] == key[None, :]
    mix = jnp.where(pick, w_key[None, :], 0.0).astype(jnp.bfloat16)
    scale_sel = jnp.take(scale_all, jnp.maximum(src_key, 0))
    picked = jnp.dot(choose, group, preferred_element_type=jnp.float32)
    outgoing = picked * scale_sel[:, None] * norm_gain + jnp.sum(mix) * 0
    outgoing = outgoing.astype(jnp.bfloat16)
    arrived = lax.all_to_all(outgoing, "rep", split_axis=0, concat_axis=0, tiled=True)
    results = run_expert(arrived, w_gate, w_up, w_down)
    results = results + jnp.sum(mix) * 0
    returned = lax.all_to_all(results, "rep", split_axis=0, concat_axis=0, tiled=True)
    partial = jnp.dot(mix, returned, preferred_element_type=jnp.float32)
    mixed = lax.psum_scatter(partial.astype(jnp.bfloat16), "exp", scatter_dimension=0, tiled=True)
    return mixed


def solution(mesh):
    placed = (
        P(("rep", "exp"), None),
        P(("rep", "exp")),
        P(("rep", "exp"), None),
        P(("rep", "exp"), None),
        P(("rep", "exp")),
        P(),
        P(("rep", "exp"), None, None),
        P(("rep", "exp"), None, None),
        P(("rep", "exp"), None, None),
    )
    return jax.shard_map(
        shards, mesh=mesh, in_specs=placed, out_specs=P(("rep", "exp"), None), check_vma=False
    )
```

profile of v0, /device:TPU:1, one launch (start us, length us, event | category | flops | bytes accessed | tf_op | source)
XLA Modules:
  0.0 427.1 jit_solution(2725431339173172228)
XLA Ops:
  6.5 0.7 all-gather.3.cloned.1.call-update
  7.3 0.8 copy.36
  9.1 0.7 reduce_sum.73
  9.8 0.7 divide_multiply_fusion
  10.8 0.7 broadcast_in_dim.91
  11.7 0.3 fusion.20
  12.3 0.5 fusion.19
  12.8 1.2 select_reduce_fusion.2
  14.2 0.8 fusion.6
  15.1 0.7 select_reduce_fusion
  16.1 17.8 %all_gather.9 = f32[16,8,8,10,3]{0,2,4,3,1:T(8,128)S(1)} all-gather(f32[16,1,8,10,3]{0,2,4,3,1:T(8,128)S(1)} %copy.41), channel_id=1, replica_groups=mesh['rep'=16,'exp'=8] {'exp'}, dimensions={1}, use_global_device_ids=true | all-gather | bytes 138240 | tf_op jit(solution)/shard_map/all_gather | solution.py:54
  34.6 1.9 fusion.14
  38.1 10.9 %all-gather = f32[8,1,128]{2,1,0:T(1,128)S(1)} all-gather(f32[1,1,128]{2,1,0:T(1,128)S(1)} %rsqrt_bitcast_fusion), channel_id=1, replica_groups=mesh['rep'=16,'exp'=8] {'exp'}, dimensions={0}, use_global_device_ids=true | all-gather | bytes 4608 | tf_op jit(solution)/shard_map/all_gather | solution.py:53
  49.1 5.0 %gather_fusion = f32[1280]{0:T(1024)S(1)} fusion(f32[1024]{0:T(1024)S(1)} %bitcast.60, s32[2048]{0:T(1024)S(1)} %pad_clamp_fusion), kind=kCustom, calls=%fused_computation | custom fusion | bytes 15360 | tf_op jit(solution)/shard_map/jit(_take)/gather | solution.py:67
  54.0 0.5 fusion.7
  54.5 10.2 %all-gather.3.cloned.1.call-done = bf16[1024,4096]{1,0:T(8,128)(2,1)} async-done(((bf16[128,4096]{1,0:T(8,128)(2,1)}), bf16[1024,4096]{1,0:T(8,128)(2,1)}) %all-gather.3.cloned.1.call-update) | async-done | bytes 8388624 | tf_op jit(solution)/shard_map/all_gather | solution.py:50
  64.8 13.7 %add_convert_fusion = bf16[1280,4096]{1,0:T(8,128)(2,1)S(1)} fusion(bf16[1280,1024]{1,0:T(8,128)(2,1)S(1)} %fusion.7, bf16[1024,4096]{1,0:T(8,128)(2,1)} %all-gather.3.cloned.1.call-done, f32[]{:T(128)S(6)} %convert_element_type.136, f32[4096]{0:T(1024)S(1)} %copy-done.1, f32[1280]{0:T(1024)S(1)} %get-tuple-element.7), kind=kOutput, calls=%fused_computation.1 | convolution fusion | flops 10758389760 | bytes 21517316 | tf_op jit(solution)/shard_map/dot_general | solution.py:68
  78.5 123.9 %all_to_all.24 = bf16[16,80,4096]{2,1,0:T(8,128)(2,1)S(1)} all-to-all(bf16[16,80,4096]{2,1,0:T(8,128)(2,1)S(1)} %bitcast.61), channel_id=1, replica_groups=mesh['rep'=16,'exp'=8] {'rep'}, dimensions={0} | all-to-all | bytes 20971520 | tf_op jit(solution)/shard_map/all_to_all | solution.py:71
  202.4 12.5 %fusion.4 = f32[1280,768]{1,0:T(8,128)S(1)} fusion(bf16[1280,4096]{1,0:T(8,128)(2,1)S(1)} %bitcast.63, bf16[1,4096,768]{2,1,0:T(8,128)(2,1)} %param.15), kind=kOutput, calls=%fused_computation.8 | convolution fusion | flops 8053063680 | bytes 20709376 | tf_op jit(solution)/shard_map/dot_general | solution.py:8
  214.9 9.8 %fusion.11 = bf16[1280,768]{1,0:T(8,128)(2,1)} fusion(bf16[1280,4096]{1,0:T(8,128)(2,1)S(1)} %bitcast.64, bf16[1,4096,768]{2,1,0:T(8,128)(2,1)S(1)} %bitcast.70, f32[1280,768]{1,0:T(8,128)S(1)} %fusion.4), kind=kOutput, calls=%fused_computation.20 | convolution fusion | flops 8058961920 | bytes 22675456 | tf_op jit(solution)/shard_map/dot_general | solution.py:9
  224.7 11.0 %fusion = bf16[1280,4096]{1,0:T(8,128)(2,1)S(1)} fusion(bf16[1280,768]{1,0:T(8,128)(2,1)} %fusion.11, bf16[1,768,4096]{2,1,0:T(8,128)(2,1)} %param.17, bf16[]{:T(256)S(6)} %mul.65), kind=kOutput, calls=%fused_computation.3 | convolution fusion | flops 8063549440 | bytes 18743298 | tf_op jit(solution)/shard_map/dot_general | solution.py:11
  235.8 119.5 %all_to_all.25 = bf16[16,80,4096]{2,1,0:T(8,128)(2,1)S(1)} all-to-all(bf16[16,80,4096]{2,1,0:T(8,128)(2,1)S(1)} %bitcast.65), channel_id=1, replica_groups=mesh['rep'=16,'exp'=8] {'rep'}, dimensions={0} | all-to-all | bytes 20971520 | tf_op jit(solution)/shard_map/all_to_all | solution.py:74
  355.3 13.0 %convolution_convert_fusion.1 = bf16[1024,4096]{1,0:T(8,128)(2,1)} fusion(bf16[1280,4096]{1,0:T(8,128)(2,1)S(1)} %bitcast.62, bf16[1280]{0:T(1024)(128)(2,1)S(1)} %broadcast_in_dim.97, s32[1280]{0:T(1024)S(1)} %convert_element_type.130), kind=kOutput, calls=%fused_computation.4 | convolution fusion | flops 10744233984 | bytes 18882048 | tf_op jit(solution)/shard_map/dot_general | solution.py:75
  368.3 51.9 %reduce-scatter.2.cloned.1.call-done = bf16[128,4096]{1,0:T(8,128)(2,1)} async-done(((bf16[1024,4096]{1,0:T(8,128)(2,1)}), bf16[128,4096]{1,0:T(8,128)(2,1)}) %reduce-scatter.2.cloned.1.call-update) | async-done | bytes 1048592 | tf_op jit(solution)/shard_map/reduce_scatter | solution.py:76
  (54 shorter events, 3.2 us)
Async XLA Ops:
  6.5 31.3 %copy-start = (bf16[128,4096]{1,0:T(8,128)(2,1)S(1)}, bf16[128,4096]{1,0:T(8,128)(2,1)}, u32[]{:S(2)}) copy-start(bf16[128,4096]{1,0:T(8,128)(2,1)} %param.9) | copy-start | bytes 3145732
  6.5 58.2 %all-gather.3.cloned.1.call-start = ((), (), s32[]{:S(2)}) async-start(), calls=%async_computation.3 | async-start | bytes 9437184 | tf_op jit(solution)/shard_map/all_gather | solution.py:50
  7.3 413.0 %reduce-scatter.2.cloned.1.call-start = ((), (), s32[]{:S(2)}) async-start(), calls=%async_computation.4 | async-start | bytes 9437184 | tf_op jit(solution)/shard_map/reduce_scatter | solution.py:76
  49.0 15.7 %copy-start.1 = (f32[4096]{0:T(1024)S(1)}, f32[4096]{0:T(1024)}, u32[]{:S(2)}) copy-start(f32[4096]{0:T(1024)} %param.14) | copy-start | bytes 49156
  78.5 136.4 %slice-start = ((s8[6291456]{0:T(1024)(128)(4,1)}), s8[4194304]{0:T(1024)(128)(4,1)S(1)}, s32[]{:S(2)}) async-start(s8[6291456]{0:T(1024)(128)(4,1)} %bitcast.69), calls=%async_computation.5 | async-start | bytes 8388608
  202.4 12.5 %slice-start.1 = ((s8[6291456]{0:T(1024)(128)(4,1)}), s8[2097152]{0:T(1024)(128)(4,1)S(1)}, s32[]{:S(2)}) async-start(s8[6291456]{0:T(1024)(128)(4,1)} %bitcast.69), calls=%async_computation.6 | async-start | bytes 4194304
Sparse Core Ops, SparseCore 0:
  9.1 55.6 all-gather.2
  368.4 51.7 reduce-scatter.1
where the time goes:
time: 427 us
  blocking collectives  272 us (64%)
  waiting for transfers between devices  62.9 us (15%)
  matrix products  60.1 us (14%)
  between operations  15 us (4%)
  local copies, waits for them, and re-layouts  9.18 us (2%)
  other arithmetic  7.8 us (2%)
    all_to_all x1, blocking collectives, shards(): lax.all_to_all(outgoing, 'rep', split_axis=0, concat_axis=0, tiled=True)  124 us
    all_to_all x1, blocking collectives, shards(): lax.all_to_all(results, 'rep', split_axis=0, concat_axis=0, tiled=True)  119 us
    reduce_scatter x1, waiting for transfers between devices, shards(): lax.psum_scatter(partial.astype(jnp.bfloat16), 'exp', scatter_dimension=0...  51.9 us
    all_gather x1, blocking collectives, shards(): lax.all_gather(table.reshape(n_rep, n_exp, cap, 3), 'exp', axis=1, tiled=...  17.8 us
    dot_general x1, matrix products, shards(): picked = jnp.dot(choose, group, preferred_element_type=jnp.float32)  13.7 us
    dot_general x1, matrix products, shards(): partial = jnp.dot(mix, returned, preferred_element_type=jnp.float32)  13 us
    dot_general x1, matrix products, run_expert(): gate_val = jnp.dot(arrived, w_gate[0], preferred_element_type=jnp.float32)  12.5 us
    dot_general x1, matrix products, run_expert(): jnp.dot(act, w_down[0], preferred_element_type=jnp.float32)  11 us
  transfers between devices with their start and end apart: 2, of which 2 were waited for; matrix products, arithmetic and copies ran while one was open for 4% of the time, Pallas kernels for 0%

commit v1 on v0

--- a/solution.py
+++ b/solution.py
@@ -47,7 +47,9 @@
         ],
         axis=1,
     )
-    group = lax.all_gather(hidden, "exp", axis=0, tiled=True)
+    group = jnp.concatenate(
+        lax.all_to_all(jnp.stack([hidden] * lax.axis_size("exp")), "exp", 0, 0), axis=0
+    )
     own = hidden.astype(jnp.float32)
     own_scale = lax.rsqrt(jnp.mean(own * own, axis=1) + 1e-06)
     scale_all = lax.all_gather(own_scale, "exp", axis=0, tiled=True)

time: 427 us -> 503 us (1.18)
  blocking collectives: 272 us -> 349 us
  waiting for transfers between devices: 62.9 us -> 52 us
  starting transfers between devices: 0.04 us -> 6.95 us
    all_gather x1, blocking collectives: 17.8 us -> 97.2 us  [shards(): lax.all_gather(table.reshape(n_rep, n_exp, cap, 3), 'exp', axis=1, tiled=...]
    all_gather x1 -> x0, waiting for transfers between devices: 10.2 us -> none  [shards(): group = lax.all_gather(hidden, 'exp', axis=0, tiled=True)]
    all_to_all x0 -> x1, starting transfers between devices: none -> 6.95 us  [shards(): lax.all_to_all(jnp.stack([hidden] * lax.axis_size('exp')), 'exp', 0, 0)]
    another operation x3 -> x4, local copies, waits for them, and re-layouts: 0.11 us -> 5.59 us  [the longest x1 5.48 us: shards(): jnp.stack([hidden] * lax.axis_size('exp'))]
  transfers between devices with their start and end apart: 2 -> 2, of which waited for: 2 -> 1; matrix products, arithmetic and copies ran while one was open for 4% -> 3% of each run, Pallas kernels for 0% -> 0%
where the time goes in v1:
time: 503 us
  blocking collectives  349 us (69%)
  matrix products  60.1 us (12%)
  waiting for transfers between devices  52 us (10%)
  between operations  15.1 us (3%)
  local copies, waits for them, and re-layouts  13.3 us (3%)
  starting transfers between devices  6.95 us (1%)
  other arithmetic  6.43 us (1%)
    all_to_all x1, blocking collectives, shards(): lax.all_to_all(outgoing, 'rep', split_axis=0, concat_axis=0, tiled=True)  124 us
    all_to_all x1, blocking collectives, shards(): lax.all_to_all(results, 'rep', split_axis=0, concat_axis=0, tiled=True)  120 us
    all_gather x1, blocking collectives, shards(): lax.all_gather(table.reshape(n_rep, n_exp, cap, 3), 'exp', axis=1, tiled=...  97.2 us
    reduce_scatter x1, waiting for transfers between devices, shards(): lax.psum_scatter(partial.astype(jnp.bfloat16), 'exp', scatter_dimension=0...  52 us
    dot_general x1, matrix products, shards(): picked = jnp.dot(choose, group, preferred_element_type=jnp.float32)  13.7 us
    dot_general x1, matrix products, shards(): partial = jnp.dot(mix, returned, preferred_element_type=jnp.float32)  13 us
    dot_general x1, matrix products, run_expert(): gate_val = jnp.dot(arrived, w_gate[0], preferred_element_type=jnp.float32)  12.5 us
    dot_general x1, matrix products, run_expert(): jnp.dot(act, w_down[0], preferred_element_type=jnp.float32)  11 us
  transfers between devices with their start and end apart: 2, of which 1 were waited for; matrix products, arithmetic and copies ran while one was open for 3% of the time, Pallas kernels for 0%

profile of v1, /device:TPU:1, one launch (start us, length us, event | category | flops | bytes accessed | tf_op | source)
XLA Modules:
  0.0 503.0 jit_solution(17387646995896650337)
XLA Ops:
  6.5 5.5 %stack.8 = bf16[8,128,4096]{2,1,0:T(8,128)(2,1)} broadcast(bf16[128,4096]{1,0:T(8,128)(2,1)} %param.9), dimensions={1,2} | broadcast | bytes 9437184 | tf_op jit(solution)/shard_map/stack | solution.py:51
  12.0 6.9 %all-to-all-start = ((bf16[8,128,4096]{2,1,0:T(8,128)(2,1)}), bf16[8,128,4096]{2,1,0:T(8,128)(2,1)}, u32[]{:S(2)}, u32[]{:S(2)}) async-start(bf16[8,128,4096]{2,1,0:T(8,128)(2,1)} %stack.8), calls=%async_computation | async-start | bytes 16777216 | tf_op jit(solution)/shard_map/all_to_all | solution.py:51
  20.7 0.3 fusion.20
  21.3 0.5 fusion.19
  21.8 1.2 select_reduce_fusion.2
  23.2 0.8 fusion.6
  24.1 0.7 select_reduce_fusion
  24.9 0.2 copy.41
  25.2 97.2 %all_gather.6 = f32[16,8,8,10,3]{0,2,4,3,1:T(8,128)S(1)} all-gather(f32[16,1,8,10,3]{0,2,4,3,1:T(8,128)S(1)} %copy.41), channel_id=1, replica_groups=mesh['rep'=16,'exp'=8] {'exp'}, dimensions={1}, use_global_device_ids=true | all-gather | bytes 138240 | tf_op jit(solution)/shard_map/all_gather | solution.py:56
  122.5 0.1 copy.44
  122.7 0.1 broadcast_in_dim.97
  123.1 1.9 fusion.14
  126.3 0.3 multiply_reduce_fusion
  126.6 8.5 %all-gather = f32[8,1,128]{2,1,0:T(1,128)S(1)} all-gather(f32[1,1,128]{2,1,0:T(1,128)S(1)} %rsqrt_bitcast_fusion), channel_id=1, replica_groups=mesh['rep'=16,'exp'=8] {'exp'}, dimensions={0}, use_global_device_ids=true | all-gather | bytes 4608 | tf_op jit(solution)/shard_map/all_gather | solution.py:55
  135.0 5.0 gather_fusion
  140.0 0.5 fusion.7
  140.6 13.7 %add_convert_fusion = bf16[1280,4096]{1,0:T(8,128)(2,1)S(1)} fusion(bf16[1280,1024]{1,0:T(8,128)(2,1)S(1)} %fusion.7, bf16[1024,4096]{1,0:T(8,128)(2,1)} %bitcast.6, f32[]{:T(128)S(6)} %convert_element_type.136, f32[4096]{0:T(1024)S(1)} %copy-done.4, f32[1280]{0:T(1024)S(1)} %get-tuple-element.7), kind=kOutput, calls=%fused_computation.1 | convolution fusion | flops 10758389760 | bytes 21517316 | tf_op jit(solution)/shard_map/dot_general | solution.py:70
  154.3 123.8 %all_to_all.29 = bf16[16,80,4096]{2,1,0:T(8,128)(2,1)S(1)} all-to-all(bf16[16,80,4096]{2,1,0:T(8,128)(2,1)S(1)} %bitcast.62), channel_id=1, replica_groups=mesh['rep'=16,'exp'=8] {'rep'}, dimensions={0} | all-to-all | bytes 20971520 | tf_op jit(solution)/shard_map/all_to_all | solution.py:73
  278.1 12.5 %fusion.4 = f32[1280,768]{1,0:T(8,128)S(1)} fusion(bf16[1280,4096]{1,0:T(8,128)(2,1)S(1)} %bitcast.64, bf16[1,4096,768]{2,1,0:T(8,128)(2,1)} %param.15), kind=kOutput, calls=%fused_computation.8 | convolution fusion | flops 8053063680 | bytes 20709376 | tf_op jit(solution)/shard_map/dot_general | solution.py:8
  290.6 9.8 %fusion.11 = bf16[1280,768]{1,0:T(8,128)(2,1)} fusion(bf16[1280,4096]{1,0:T(8,128)(2,1)S(1)} %bitcast.65, bf16[1,4096,768]{2,1,0:T(8,128)(2,1)S(1)} %bitcast.71, f32[1280,768]{1,0:T(8,128)S(1)} %fusion.4), kind=kOutput, calls=%fused_computation.20 | convolution fusion | flops 8058961920 | bytes 22675456 | tf_op jit(solution)/shard_map/dot_general | solution.py:9
  300.5 11.0 %fusion = bf16[1280,4096]{1,0:T(8,128)(2,1)S(1)} fusion(bf16[1280,768]{1,0:T(8,128)(2,1)} %fusion.11, bf16[1,768,4096]{2,1,0:T(8,128)(2,1)} %param.17, bf16[]{:T(256)S(6)} %mul.65), kind=kOutput, calls=%fused_computation.3 | convolution fusion | flops 8063549440 | bytes 18743298 | tf_op jit(solution)/shard_map/dot_general | solution.py:11
  311.5 119.5 %all_to_all.30 = bf16[16,80,4096]{2,1,0:T(8,128)(2,1)S(1)} all-to-all(bf16[16,80,4096]{2,1,0:T(8,128)(2,1)S(1)} %bitcast.66), channel_id=1, replica_groups=mesh['rep'=16,'exp'=8] {'rep'}, dimensions={0} | all-to-all | bytes 20971520 | tf_op jit(solution)/shard_map/all_to_all | solution.py:76
  431.1 13.0 %convolution_convert_fusion.1 = bf16[1024,4096]{1,0:T(8,128)(2,1)} fusion(bf16[1280,4096]{1,0:T(8,128)(2,1)S(1)} %bitcast.63, bf16[1280]{0:T(1024)(128)(2,1)S(1)} %broadcast_in_dim.97, s32[1280]{0:T(1024)S(1)} %convert_element_type.130), kind=kOutput, calls=%fused_computation.4 | convolution fusion | flops 10744233984 | bytes 18882048 | tf_op jit(solution)/shard_map/dot_general | solution.py:77
  444.1 52.0 %reduce-scatter.2.cloned.1.call-done = bf16[128,4096]{1,0:T(8,128)(2,1)} async-done(((bf16[1024,4096]{1,0:T(8,128)(2,1)}), bf16[128,4096]{1,0:T(8,128)(2,1)}) %reduce-scatter.2.cloned.1.call-update) | async-done | bytes 1048592 | tf_op jit(solution)/shard_map/reduce_scatter | solution.py:78
  (60 shorter events, 2.6 us)
Async XLA Ops:
  12.0 7.0 %copy-start.2 = (s32[128,8]{0,1:T(8,128)S(1)}, s32[128,8]{0,1:T(8,128)}, u32[]{:S(2)}) copy-start(s32[128,8]{0,1:T(8,128)} %param.11) | copy-start | bytes 12292
  12.0 8.1 %copy-start.1 = (f32[128,8]{0,1:T(8,128)S(1)}, f32[128,8]{0,1:T(8,128)}, u32[]{:S(2)}) copy-start(f32[128,8]{0,1:T(8,128)} %param.12) | copy-start | bytes 12292
  12.0 8.5 %copy-start.3 = (s32[128]{0:T(128)S(1)}, s32[128]{0:T(128)}, u32[]{:S(2)}) copy-start(s32[128]{0:T(128)} %param.10) | copy-start | bytes 1540
  12.0 128.5 %all-to-all-start = ((bf16[8,128,4096]{2,1,0:T(8,128)(2,1)}), bf16[8,128,4096]{2,1,0:T(8,128)(2,1)}, u32[]{:S(2)}, u32[]{:S(2)}) async-start(bf16[8,128,4096]{2,1,0:T(8,128)(2,1)} %stack.8), calls=%async_computation | async-start | bytes 16777216 | tf_op jit(solution)/shard_map/all_to_all | solution.py:51
  19.0 107.3 %copy-start = (bf16[128,4096]{1,0:T(8,128)(2,1)S(1)}, bf16[128,4096]{1,0:T(8,128)(2,1)}, u32[]{:S(2)}) copy-start(bf16[128,4096]{1,0:T(8,128)(2,1)} %param.9) | copy-start | bytes 3145732
  19.0 477.2 %reduce-scatter.2.cloned.1.call-start = ((), (), s32[]{:S(2)}) async-start(), calls=%async_computation.4 | async-start | bytes 9437184 | tf_op jit(solution)/shard_map/reduce_scatter | solution.py:78
  135.0 5.5 %copy-start.4 = (f32[4096]{0:T(1024)S(1)}, f32[4096]{0:T(1024)}, u32[]{:S(2)}) copy-start(f32[4096]{0:T(1024)} %param.14) | copy-start | bytes 49156
  154.3 136.3 %slice-start = ((s8[6291456]{0:T(1024)(128)(4,1)}), s8[4194304]{0:T(1024)(128)(4,1)S(1)}, s32[]{:S(2)}) async-start(s8[6291456]{0:T(1024)(128)(4,1)} %bitcast.70), calls=%async_computation.5 | async-start | bytes 8388608
  278.1 12.5 %slice-start.1 = ((s8[6291456]{0:T(1024)(128)(4,1)}), s8[2097152]{0:T(1024)(128)(4,1)S(1)}, s32[]{:S(2)}) async-start(s8[6291456]{0:T(1024)(128)(4,1)} %bitcast.70), calls=%async_computation.6 | async-start | bytes 4194304
Sparse Core Ops, SparseCore 0:
  444.2 51.8 reduce-scatter.1
